TPU v7x, 32 devices: a whole 2x2x4 slice. The times are simulated.
32 devices in a mesh: seq: 8 (over y, x, core), wt: 4 (over z).
Axes of the slice: x: 2, y: 2, z: 4, core: 2. Of those that a mesh axis runs over, the one named last changes fastest.
Arguments:
- inputs: bfloat16 [8, 1024, 1024], P('wt', 'seq'), may hold values from -5 to 5
- cotangent: bfloat16 [8, 1024, 1024], P('wt', 'seq'), may hold values from -6 to 6
- decay: float32 [8, 1024, 8], P('wt', 'seq'), may hold values from 0.3 to 1
- w_query: bfloat16 [1024, 1024], P('wt'), may hold values from -0.1875 to 0.1875
- w_key: bfloat16 [1024, 1024], P('wt'), may hold values from -0.1875 to 0.1875
- w_value: bfloat16 [1024, 2048], P('wt'), may hold values from -0.1875 to 0.1875
- w_gate_out: bfloat16 [1024, 2048], P('wt'), may hold values from -0.1875 to 0.1875
- w_out: bfloat16 [1024, 2048], P('wt'), may hold values from -0.125 to 0.125
- w_ffn_gate: bfloat16 [1024, 2816], P('wt'), may hold values from -0.1875 to 0.1875
- w_ffn_up: bfloat16 [1024, 2816], P('wt'), may hold values from -0.1875 to 0.1875
- w_ffn_down: bfloat16 [1024, 2816], P('wt'), may hold values from -0.109375 to 0.109375
- w_beta: bfloat16 [1024, 8], replicated, may hold values from -1 to 1
- conv_weight: float32 [4, 4096], replicated, may hold values from -3 to 3
- norm_in: float32 [1024], replicated, may hold values from 0.5 to 1.5
- norm_mid: float32 [1024], replicated, may hold values from 0.5 to 1.5
- norm_head: float32 [256], replicated, may hold values from 0.5 to 1.5
Outputs:
- layer_out: bfloat16 [8, 1024, 1024], P('wt', 'seq')
- grad_input: float32 [8, 1024, 1024], P('wt', 'seq')
- grad_query: float32 [1024, 1024], P('wt')
- grad_key: float32 [1024, 1024], P('wt')
- grad_value: float32 [1024, 2048], P('wt')
- grad_gate_out: float32 [1024, 2048], P('wt')
- grad_out: float32 [1024, 2048], P('wt')
- slope_feedforward_switch: float32 [1024, 2816], P('wt')
- grad_ffn_up: float32 [1024, 2816], P('wt')
- grad_ffn_down: float32 [1024, 2816], P('wt')
- grad_beta: float32 [1024, 8], replicated
- grad_conv: float32 [4, 4096], replicated
- grad_norm_in: float32 [1024], replicated
- grad_norm_mid: float32 [1024], replicated
- grad_norm_head: float32 [256], replicated
All inputs are finite; a program needn't handle non-finite values.
Results may differ from a plain program's by a relative error of at most 0.0095.
The roundings to bfloat16 on the way count: a program that leaves them out, or rounds other values in their place, can miss the bound.
Values may be sent and summed in bfloat16 or wider, within the bound.
No kernel may reach another device: no remote copies, remote signals or barrier semaphores. Data moves between devices by JAX's collectives and lax.ppermute only.
A program may use at most 320 MiB of HBM per device.

v0:
```python
import jax
import jax.numpy as jnp
from jax import lax
from jax.sharding import PartitionSpec as P

H = 8
DK = 128
DV = 256
FF = 2816
CONV = 4
GROUP = 64
highest = lax.Precision.HIGHEST


def passed_along(array, axis, by):
    peers = lax.axis_size(axis)
    pairs = [(i, i + by) for i in range(peers) if 0 <= i + by < peers]
    return lax.ppermute(array, axis, pairs)


def product(left, right):
    return jnp.dot(left, right, preferred_element_type=jnp.float32)


def contract_rows(left, right):
    return lax.dot_general(
        left, right, (((0,), (0,)), ((), ())), preferred_element_type=jnp.float32
    )


def contract_cols(left, right):
    return lax.dot_general(
        left, right, (((1,), (1,)), ((), ())), preferred_element_type=jnp.float32
    )


def rms_norm(values, scaling):
    return values * lax.rsqrt(jnp.mean(values * values, axis=-1, keepdims=True) + 1e-05) * scaling


def head_norm(mixed, out_gate, scaling):
    multiplier_coefficient = lax.rsqrt(jnp.mean(mixed * mixed, axis=-1, keepdims=True) + 1e-05)
    gate_heads = out_gate.reshape(mixed.shape)
    return (mixed * multiplier_coefficient * scaling * jax.nn.silu(gate_heads)).reshape(
        out_gate.shape
    )


def pre_mix(padded, conv_weight, beta_logit):
    length = padded.shape[1] - (CONV - 1)
    summed = padded[:, 0:length] * conv_weight[0]
    for tap_index in range(1, CONV):
        summed = summed + padded[:, tap_index : tap_index + length] * conv_weight[tap_index]
    active = jax.nn.silu(summed)
    leading = active.shape[:2]
    queries = active[..., : H * DK].reshape(leading + (H, DK))
    keys_raw = active[..., H * DK : 2 * H * DK].reshape(leading + (H, DK))
    keys_unit = keys_raw * lax.rsqrt(jnp.sum(keys_raw * keys_raw, axis=-1, keepdims=True) + 1e-06)
    values = active[..., 2 * H * DK :].reshape(leading + (H, DV))
    return (queries, keys_unit, values, jax.nn.sigmoid(beta_logit))


def group_step(state, pieces):
    queries, keys_unit, values, betas, log_decay = pieces
    length = queries.shape[1]
    row_ids = lax.broadcasted_iota(jnp.int32, (length, length), 0)
    col_ids = lax.broadcasted_iota(jnp.int32, (length, length), 1)
    causal = row_ids >= col_ids
    strict = row_ids > col_ids
    running = jnp.cumsum(log_decay, axis=1)
    value_spread = jnp.where(causal, running[:, :, None] - running[:, None, :], 0.0)
    decay_mat = jnp.where(causal, jnp.exp(value_spread), 0.0)
    key_gram = jnp.einsum("hid,hjd->hij", keys_unit, keys_unit, precision=highest)
    system = jnp.eye(length, dtype=state.dtype) + jnp.where(
        strict, betas[:, :, None] * key_gram * decay_mat, 0.0
    )
    growth = jnp.exp(running)
    recalled = jnp.einsum("hid,hde->hie", keys_unit, state, precision=highest)
    target = betas[:, :, None] * (values - growth[:, :, None] * recalled)
    deltas = jax.scipy.linalg.solve_triangular(system, target, lower=True, unit_diagonal=True)
    scores = jnp.einsum("hid,hjd->hij", queries, keys_unit, precision=highest) * decay_mat
    read_out = growth[:, :, None] * jnp.einsum("hid,hde->hie", queries, state, precision=highest)
    read_out = read_out + jnp.einsum("hij,hje->hie", scores, deltas, precision=highest)
    final_log = running[:, -1:]
    weights_in = jnp.exp(final_log - running)
    new_state = jnp.exp(final_log)[:, :, None] * state + jnp.einsum(
        "hid,hie->hde", keys_unit * weights_in[:, :, None], deltas, precision=highest
    )
    return (new_state, read_out)


def delta_rule(state, queries, keys_unit, values, betas, log_decay):
    length = queries.shape[0]
    blocks = length // GROUP

    def arrange(array):
        return jnp.swapaxes(array.reshape((blocks, GROUP) + array.shape[1:]), 1, 2)

    final_state, read_out = lax.scan(
        jax.checkpoint(group_step),
        state,
        (arrange(queries), arrange(keys_unit), arrange(values), arrange(betas), arrange(log_decay)),
    )
    ordered = jnp.swapaxes(read_out, 1, 2)
    return (ordered.reshape((length,) + ordered.shape[2:]), final_state)


def shards(
    inputs,
    cotangent,
    decay,
    w_query,
    w_key,
    w_value,
    w_gate_out,
    w_out,
    w_ffn_gate,
    w_ffn_up,
    w_ffn_down,
    w_beta,
    conv_weight,
    norm_in,
    norm_mid,
    norm_head,
):
    seq_count, block_len, model_width = inputs.shape
    row_count = seq_count * block_len
    edge_rows = CONV - 1
    head_keys = H * DK
    head_values = H * DV
    (
        full_query,
        full_key,
        full_value,
        full_gate,
        full_out,
        full_ffn_gate,
        full_ffn_up,
        full_ffn_down,
    ) = (
        lax.all_gather(w_query, "wt", axis=0, tiled=True),
        lax.all_gather(w_key, "wt", axis=0, tiled=True),
        lax.all_gather(w_value, "wt", axis=0, tiled=True),
        lax.all_gather(w_gate_out, "wt", axis=0, tiled=True),
        lax.all_gather(w_out, "wt", axis=0, tiled=True),
        lax.all_gather(w_ffn_gate, "wt", axis=0, tiled=True),
        lax.all_gather(w_ffn_up, "wt", axis=0, tiled=True),
        lax.all_gather(w_ffn_down, "wt", axis=0, tiled=True),
    )
    flat_in = inputs.reshape(row_count, model_width).astype(jnp.float32)
    normed_first, norm_back_in = jax.vjp(rms_norm, flat_in, norm_in)
    normed_in = normed_first.astype(jnp.bfloat16)
    conv_in = jnp.concatenate(
        [
            product(normed_in, full_query),
            product(normed_in, full_key),
            product(normed_in, full_value),
        ],
        axis=1,
    ).astype(jnp.bfloat16)
    out_gate = product(normed_in, full_gate)
    beta_logit = product(normed_in, w_beta)
    conv_blocks = conv_in.reshape(seq_count, block_len, -1)
    before_rows = passed_along(conv_blocks[:, block_len - edge_rows :], "seq", 1)
    padded = jnp.concatenate([before_rows, conv_blocks], axis=1).astype(jnp.float32)
    (queries, keys_unit, values, betas), pre_back = jax.vjp(
        pre_mix, padded, conv_weight, beta_logit.reshape(seq_count, block_len, H)
    )
    log_decay = jnp.log(decay)
    eye_state = jnp.broadcast_to(jnp.eye(DK, dtype=jnp.float32), (seq_count, H, DK, DK))
    zero_state = jnp.zeros((seq_count, H, DK, DV), jnp.float32)
    run_rule = jax.vmap(delta_rule)
    transfer = run_rule(eye_state, queries, keys_unit, jnp.zeros_like(keys_unit), betas, log_decay)[
        1
    ]
    local_end = run_rule(zero_state, queries, keys_unit, values, betas, log_decay)[1]

    def forward_turn(turn_index, carried):
        moved = jnp.einsum("shij,shjk->shik", transfer, carried, precision=highest) + local_end
        return passed_along(moved, "seq", 1)

    start_state = lax.fori_loop(0, lax.axis_size("seq") - 1, forward_turn, zero_state)

    def mixer(state_in, query_in, key_in, value_in, beta_in):
        return run_rule(state_in, query_in, key_in, value_in, beta_in, log_decay)

    mixer_output, mixer_back = jax.vjp(mixer, start_state, queries, keys_unit, values, betas)
    mixed = mixer_output[0]
    headed_full, head_back = jax.vjp(
        head_norm, mixed, out_gate.reshape(seq_count, block_len, head_values), norm_head
    )
    headed = headed_full.reshape(row_count, head_values).astype(jnp.bfloat16)
    residual = flat_in + contract_cols(headed, full_out)
    normed_second, norm_back_mid = jax.vjp(rms_norm, residual, norm_mid)
    normed_mid = normed_second.astype(jnp.bfloat16)
    gate_pre = product(normed_mid, full_ffn_gate)
    up_pre = product(normed_mid, full_ffn_up)
    sigmoid_gate = jax.nn.sigmoid(gate_pre)
    swish_gate = gate_pre * sigmoid_gate
    hidden = (swish_gate * up_pre).astype(jnp.bfloat16)
    layer_out = (
        (residual + contract_cols(hidden, full_ffn_down))
        .astype(jnp.bfloat16)
        .reshape(seq_count, block_len, model_width)
    )
    upstream = cotangent.reshape(row_count, model_width)
    inner_feedforward_width = product(upstream, full_ffn_down)
    d_gate = (
        inner_feedforward_width * up_pre * sigmoid_gate * (1.0 + gate_pre * (1.0 - sigmoid_gate))
    ).astype(jnp.bfloat16)
    d_up = (inner_feedforward_width * swish_gate).astype(jnp.bfloat16)
    left_rows = normed_mid
    outer_rows = upstream
    ffn_share = lax.psum_scatter(
        jnp.concatenate(
            [
                contract_rows(left_rows, d_gate),
                contract_rows(left_rows, d_up),
                contract_rows(outer_rows, hidden),
            ],
            axis=1,
        ),
        "wt",
        scatter_dimension=0,
        tiled=True,
    )
    d_normed_mid = contract_cols(d_gate, full_ffn_gate) + contract_cols(d_up, full_ffn_up)
    d_from_mid, middle_gradient = norm_back_mid(d_normed_mid)
    d_residual = upstream.astype(jnp.float32) + d_from_mid
    d_branch = d_residual.astype(jnp.bfloat16)
    dimension_across_heads = product(d_branch, full_out)
    d_mixed, d_out_gate, grad_head = head_back(
        dimension_across_heads.reshape(seq_count, block_len, head_values)
    )
    local_start = mixer_back((d_mixed, zero_state))[0]
    transposed = jnp.swapaxes(transfer, 2, 3)

    def backward_turn(turn_index, carried):
        moved = jnp.einsum("shij,shjk->shik", transposed, carried, precision=highest) + local_start
        return passed_along(moved, "seq", -1)

    end_grad = lax.fori_loop(0, lax.axis_size("seq") - 1, backward_turn, zero_state)
    mixer_grads = mixer_back((d_mixed, end_grad))
    d_padded, grad_conv, d_beta_logit = pre_back(
        (mixer_grads[1], mixer_grads[2], mixer_grads[3], mixer_grads[4])
    )
    after_rows = passed_along(d_padded[:, :edge_rows], "seq", -1)
    d_conv_in = d_padded[:, edge_rows:] + jnp.pad(
        after_rows, ((0, 0), (block_len - edge_rows, 0), (0, 0))
    )
    d_conv_flat = d_conv_in.reshape(row_count, -1).astype(jnp.bfloat16)
    d_gate_flat = d_out_gate.reshape(row_count, head_values).astype(jnp.bfloat16)
    d_beta_flat = d_beta_logit.reshape(row_count, H).astype(jnp.bfloat16)
    left_rows = normed_in
    outer_rows = d_branch
    mixer_share = lax.psum_scatter(
        jnp.concatenate(
            [
                contract_rows(left_rows, d_conv_flat),
                contract_rows(left_rows, d_gate_flat),
                contract_rows(outer_rows, headed),
            ],
            axis=1,
        ),
        "wt",
        scatter_dimension=0,
        tiled=True,
    )
    grad_beta = contract_rows(normed_in, d_beta_flat)
    d_normed_in = contract_cols(d_conv_flat[:, :head_keys], full_query) + contract_cols(
        d_conv_flat[:, head_keys : 2 * head_keys], full_key
    )
    d_normed_in = (
        d_normed_in
        + contract_cols(d_conv_flat[:, 2 * head_keys :], full_value)
        + contract_cols(d_gate_flat, full_gate)
    )
    d_normed_in = d_normed_in + contract_cols(d_beta_flat, w_beta)
    d_from_in, grad_in = norm_back_in(d_normed_in)
    grad_input = (d_residual + d_from_in).reshape(seq_count, block_len, model_width)
    mixer_sum, ffn_sum = lax.psum((mixer_share, ffn_share), "seq")
    grad_beta, grad_conv, grad_in, middle_gradient, grad_head = lax.psum(
        (grad_beta, grad_conv, grad_in, middle_gradient, grad_head), ("seq", "wt")
    )
    value_end = 2 * head_keys + head_values
    gate_end = value_end + head_values
    return (
        layer_out,
        grad_input,
        mixer_sum[:, :head_keys],
        mixer_sum[:, head_keys : 2 * head_keys],
        mixer_sum[:, 2 * head_keys : value_end],
        mixer_sum[:, value_end:gate_end],
        mixer_sum[:, gate_end:],
        ffn_sum[:, :FF],
        ffn_sum[:, FF : 2 * FF],
        ffn_sum[:, 2 * FF :],
        grad_beta,
        grad_conv,
        grad_in,
        middle_gradient,
        grad_head,
    )


def solution(mesh):
    in_specs = (
        P("wt", "seq", None),
        P("wt", "seq", None),
        P("wt", "seq", None),
        P("wt", None),
        P("wt", None),
        P("wt", None),
        P("wt", None),
        P("wt", None),
        P("wt", None),
        P("wt", None),
        P("wt", None),
        P(),
        P(),
        P(),
        P(),
        P(),
    )
    out_specs = (
        P("wt", "seq", None),
        P("wt", "seq", None),
        P("wt", None),
        P("wt", None),
        P("wt", None),
        P("wt", None),
        P("wt", None),
        P("wt", None),
        P("wt", None),
        P("wt", None),
        P(),
        P(),
        P(),
        P(),
        P(),
    )
    return jax.shard_map(shards, mesh=mesh, in_specs=in_specs, out_specs=out_specs, check_vma=False)
```

profile of v0, /device:TPU:1, one launch (start us, length us, event | category | flops | bytes accessed | tf_op | source)
XLA Modules:
  0.0 3432.0 jit_solution(14489899089912197021)
XLA Ops:
  13.6 44.1 %all-gather.11.cloned.1.call-done = bf16[1024,1024]{1,0:T(8,128)(2,1)} async-done(((bf16[256,1024]{1,0:T(8,128)(2,1)}), bf16[1024,1024]{1,0:T(8,128)(2,1)}) %all-gather.11.cloned.1.call-update) | async-done | bytes 2097168 | tf_op jit(solution)/shard_map/all_gather | solution.py:142
  60.0 43.9 %all-gather.9.cloned.1.call-done = bf16[1024,1024]{1,0:T(8,128)(2,1)} async-done(((bf16[256,1024]{1,0:T(8,128)(2,1)}), bf16[1024,1024]{1,0:T(8,128)(2,1)}) %all-gather.9.cloned.1.call-update) | async-done | bytes 2097168 | tf_op jit(solution)/shard_map/all_gather | solution.py:141
  106.2 78.8 %all-gather.13.cloned.1.call-done = bf16[1024,2048]{1,0:T(8,128)(2,1)} async-done(((bf16[256,2048]{1,0:T(8,128)(2,1)}), bf16[1024,2048]{1,0:T(8,128)(2,1)}) %all-gather.13.cloned.1.call-update) | async-done | bytes 4194320 | tf_op jit(solution)/shard_map/all_gather | solution.py:143
  193.6 72.1 %all-gather.15.cloned.1.call-done = bf16[1024,2048]{1,0:T(8,128)(2,1)} async-done(((bf16[256,2048]{1,0:T(8,128)(2,1)}), bf16[1024,2048]{1,0:T(8,128)(2,1)}) %all-gather.15.cloned.1.call-update) | async-done | bytes 4194320 | tf_op jit(solution)/shard_map/all_gather | solution.py:144
  288.0 182.4 %while.96 = (s32[]{:T(128)}, f32[2,8,128,128]{3,2,1,0:T(8,128)}, f32[2,2,8,64]{3,2,1,0:T(8,128)S(1)}, f32[2,2,8,64,128]{4,3,2,1,0:T(8,128)S(1)}, f32[2,2,8,64]{3,2,1,0:T(8,128)S(1)}, /*index=5*/s32[]{:T(128)}, f32[]{:T(128)}) while((s32[]{:T(128)}, f32[2,8,128,128]{3,2,1,0:T(8,128)}, f32[2,2,8,64]{3,2,1,0:T(8,128)S(1)}, ...), condition=%wide.region_4.5_spmd, body=%wide.region_2.4_spmd.sunk | while | flops 605712448 | bytes 15951777 | solution.py:99
  293.7 80.0 %custom-call.36 = f32[2,8,1,64,64]{3,4,2,1,0:T(8,128)} custom-call(f32[2,8,1,64,64]{4,3,2,1,0:T(8,128)} %fusion.427), custom_call_target="InvertDiagBlocksLowerTriangular" | custom-call | tf_op jit(solution)/shard_map/vmap()/while/body/eval_jaxpr/checkpoint/jit(_solve_triangular)/vmap()/triangular_solve | solution.py:80
  384.9 80.0 %custom-call.36 = f32[2,8,1,64,64]{3,4,2,1,0:T(8,128)} custom-call(f32[2,8,1,64,64]{4,3,2,1,0:T(8,128)} %fusion.427), custom_call_target="InvertDiagBlocksLowerTriangular" | custom-call | tf_op jit(solution)/shard_map/vmap()/while/body/eval_jaxpr/checkpoint/jit(_solve_triangular)/vmap()/triangular_solve | solution.py:80
  474.9 183.1 %while.101 = (s32[]{:T(128)}, f32[2,8,128,256]{3,2,1,0:T(8,128)S(1)}, f32[2,2,8,64]{3,2,1,0:T(8,128)S(1)}, f32[2,2,8,64,128]{4,3,2,1,0:T(8,128)S(1)}, f32[2,2,8,...) while((s32[]{:T(128)}, ...), condition=%wide.region_7.9_spmd.clone, body=%wide.region_5.8_spmd.clone.sunk | while | flops 1110994944 | bytes 13856127 | solution.py:99
  481.4 80.0 %custom-call.39 = f32[2,8,1,64,64]{3,4,2,1,0:T(8,128)} custom-call(f32[2,8,1,64,64]{4,3,2,1,0:T(8,128)} %fusion.505), custom_call_target="InvertDiagBlocksLowerTriangular" | custom-call | tf_op jit(solution)/shard_map/vmap()/while/body/eval_jaxpr/checkpoint/jit(_solve_triangular)/vmap()/triangular_solve/custom-call.0 | solution.py:80
  572.9 80.0 %custom-call.39 = f32[2,8,1,64,64]{3,4,2,1,0:T(8,128)} custom-call(f32[2,8,1,64,64]{4,3,2,1,0:T(8,128)} %fusion.505), custom_call_target="InvertDiagBlocksLowerTriangular" | custom-call | tf_op jit(solution)/shard_map/vmap()/while/body/eval_jaxpr/checkpoint/jit(_solve_triangular)/vmap()/triangular_solve/custom-call.0 | solution.py:80
  661.5 228.1 %while.97 = (s32[]{:T(128)}, f32[2,8,128,256]{3,2,1,0:T(8,128)S(1)}, f32[2,8,128,128]{3,2,1,0:T(8,128)}, f32[2,8,128,256]{3,2,1,0:T(8,128)}, s32[]{:T(128)}) while((s32[]{:T(128)}, f32[2,8,128,256]{3,2,1,0:T(8,128)S(1)}, f32[2,8,128,128]{3,2,1,0:T(8,128)}, f32[2,8,128,256]{3,2,1,0:T(8,128)}, s32[]{:T(128)}) %tuple.364), condition=%wide.region_9.11_spmd, body=%wide.region_8.10_spmd.sunk | while | flops 805830656 | bytes 15728741 | solution.py:182
  891.2 200.0 %while.100 = (s32[]{:T(128)}, f32[2,8,128,256]{3,2,1,0:T(8,128)S(1)}, f32[2,2,8,64,256]{4,3,2,1,0:T(8,128)}, f32[2,2,8,128,256]{4,3,2,1,0:T(8,128)}, f32[2,2,8,6...) while((s32[]{:T(128)}, ...), condition=%wide.region_12.14_spmd.clone.clone, body=%wide.region_10.13_spmd.clone.clone.sunk | while | flops 1815367680 | bytes 56082448 | solution.py:99
  901.6 80.0 %custom-call.38 = f32[2,8,1,64,64]{3,4,2,1,0:T(8,128)} custom-call(f32[2,8,1,64,64]{4,3,2,1,0:T(8,128)} %fusion.494), custom_call_target="InvertDiagBlocksLowerTriangular" | custom-call | tf_op jit(solution)/shard_map/jvp(vmap())/while/body/eval_jaxpr/jit(_solve_triangular)/vmap()/triangular_solve/custom-call.0 | solution.py:80
  1001.3 80.0 %custom-call.38 = f32[2,8,1,64,64]{3,4,2,1,0:T(8,128)} custom-call(f32[2,8,1,64,64]{4,3,2,1,0:T(8,128)} %fusion.494), custom_call_target="InvertDiagBlocksLowerTriangular" | custom-call | tf_op jit(solution)/shard_map/jvp(vmap())/while/body/eval_jaxpr/jit(_solve_triangular)/vmap()/triangular_solve/custom-call.0 | solution.py:80
  1148.8 206.5 %while.102 = (s32[]{:T(128)}, f32[2,8,128,256]{3,2,1,0:T(8,128)}, f32[2,2,8,64,128]{4,3,2,1,0:T(8,128)}, f32[2,2,8,64,128]{4,3,2,1,0:T(8,128)S(1)}, f32[2,2,8,64...) while((s32[]{:T(128)}, f32[2,8,128,256]{3,2,1,0:T(8,128)}, ...), condition=%wide.region_19.22_spmd.clone, body=%wide.region_17.21_spmd.clone.sunk | while | flops 1816424448 | bytes 58881144 | solution.py:99
  1165.5 80.0 %custom-call.40 = f32[2,8,1,64,64]{3,4,2,1,0:T(8,128)} custom-call(f32[2,8,1,64,64]{4,3,2,1,0:T(8,128)} %fusion.524), custom_call_target="InvertDiagBlocksLowerTriangular" | custom-call | tf_op jit(solution)/shard_map/transpose(jvp(vmap()))/while/body/eval_jaxpr/checkpoint/jit(_solve_triangular)/vmap()/triangular_solve/custom-call.2 | solution.py:80
  1269.1 80.0 %custom-call.40 = f32[2,8,1,64,64]{3,4,2,1,0:T(8,128)} custom-call(f32[2,8,1,64,64]{4,3,2,1,0:T(8,128)} %fusion.524), custom_call_target="InvertDiagBlocksLowerTriangular" | custom-call | tf_op jit(solution)/shard_map/transpose(jvp(vmap()))/while/body/eval_jaxpr/checkpoint/jit(_solve_triangular)/vmap()/triangular_solve/custom-call.2 | solution.py:80
  1355.6 229.8 %while.98 = (s32[]{:T(128)}, f32[2,8,128,256]{3,2,1,0:T(8,128)S(1)}, f32[2,8,128,128]{3,2,1,0:T(8,128)}, f32[2,8,128,256]{3,2,1,0:T(8,128)}, s32[]{:T(128)}) while((s32[]{:T(128)}, f32[2,8,128,256]{3,2,1,0:T(8,128)S(1)}, f32[2,8,128,128]{3,2,1,0:T(8,128)}, f32[2,8,128,256]{3,2,1,0:T(8,128)}, s32[]{:T(128)}) %tuple.370), condition=%wide.region_21.24_spmd, body=%wide.region_20.23_spmd.sunk | while | flops 805830656 | bytes 15728741 | solution.py:242
  1363.1 26.3 collective-permute-done.1
  1396.4 25.6 collective-permute-done.1
  1429.1 25.6 collective-permute-done.1
  1461.8 25.6 collective-permute-done.1
  1494.4 25.6 collective-permute-done.1
  1527.1 25.6 collective-permute-done.1
  1589.2 256.0 %while.99 = (s32[]{:T(128)}, f32[2,8,128,256]{3,2,1,0:T(8,128)S(1)}, f32[2,2,8,64,128]{4,3,2,1,0:T(8,128)}, f32[2,2,8,64,128]{4,2,3,0,1:T(8,128)}, f32[2,2,8,64,...) while((s32[]{:T(128)}, ...), condition=%wide.region_26.29_spmd, body=%wide.region_22.28_spmd.sunk | while | flops 4487867392 | bytes 149161456 | solution.py:99
  1604.1 80.0 %custom-call.37 = f32[2,8,1,64,64]{3,4,2,1,0:T(8,128)} custom-call(f32[2,8,1,64,64]{4,3,2,1,0:T(8,128)} %add_bitcast_fusion.2), custom_call_target="InvertDiagBlocksLowerTriangular" | custom-call | tf_op jit(solution)/shard_map/transpose(jvp(vmap()))/while/body/eval_jaxpr/checkpoint/jit(_solve_triangular)/vmap()/triangular_solve/custom-call.2 | solution.py:80
  1728.0 80.0 %custom-call.37 = f32[2,8,1,64,64]{3,4,2,1,0:T(8,128)} custom-call(f32[2,8,1,64,64]{4,3,2,1,0:T(8,128)} %add_bitcast_fusion.2), custom_call_target="InvertDiagBlocksLowerTriangular" | custom-call | tf_op jit(solution)/shard_map/transpose(jvp(vmap()))/while/body/eval_jaxpr/checkpoint/jit(_solve_triangular)/vmap()/triangular_solve/custom-call.2 | solution.py:80
  1978.3 519.0 %reduce-scatter.3.cloned.1.call-done = f32[256,8192]{1,0:T(8,128)} async-done(((f32[1024,8192]{1,0:T(8,128)}), f32[256,8192]{1,0:T(8,128)}) %reduce-scatter.3.cloned.1.call-update) | async-done | bytes 8388624 | tf_op jit(solution)/shard_map/reduce_scatter | solution.py:256
  2497.4 571.9 %reduce-scatter.5.cloned.1.call-done = f32[256,8448]{1,0:T(8,128)} async-done(((f32[1024,8448]{1,0:T(8,128)}), f32[256,8448]{1,0:T(8,128)}) %reduce-scatter.5.cloned.1.call-update) | async-done | bytes 8650768 | tf_op jit(solution)/shard_map/reduce_scatter | solution.py:214
  3086.5 43.4 %all-reduce.12 = (f32[1024,8]{0,1:T(8,128)}, f32[1024]{0:T(1024)}, f32[1024]{0:T(1024)}, f32[256]{0:T(256)}) all-reduce(f32[1024,8]{0,1:T(8,128)S(1)} %convolution_bitcast_fusion.2, f32[1024]{0:T(1024)S(1)} %get-tuple-element.984, f32[1024]{0:T(1024)S(1)} %copy-done.88, ...), channel_id=1, replica_groups=mesh['seq'=8,'wt'=4] {'seq','wt'}, use_global_device_ids=true, to_apply=%region_33.36 | all-reduce | flops 10496 | bytes 83968 | tf_op jit(solution)/shard_map/psum | solution.py:282
  3129.9 167.4 %all-reduce.19.cloned.1.call-done = (f32[256,8192]{1,0:T(8,128)}, f32[256,8448]{1,0:T(8,128)}) async-done(((f32[256,8192]{1,0:T(8,128)}, f32[256,8448]{1,0:T(8,128)}), (f32[256,8192]{1,0:T(8,128)}, f32[256,8448]{1,0:T(8,128)})) %all-reduce.19.cloned.1.call-update) | async-done | bytes 17039376 | tf_op jit(solution)/shard_map/psum | solution.py:281
  3311.6 111.9 %all-reduce.17.cloned.1.call-done = f32[4,4096]{1,0:T(4,128)} async-done(((f32[4,4096]{1,0:T(4,128)}), f32[4,4096]{1,0:T(4,128)}) %all-reduce.17.cloned.1.call-update) | async-done | bytes 65552 | tf_op jit(solution)/shard_map/psum | solution.py:282
  (609 shorter events, 798.9 us)
Async XLA Ops:
  7.2 50.5 %all-gather.11.cloned.1.call-start = ((), (), s32[]{:S(2)}) async-start(), calls=%async_computation.3 | async-start | bytes 2621440 | tf_op jit(solution)/shard_map/all_gather | solution.py:142
  7.9 96.0 %all-gather.9.cloned.1.call-start = ((), (), s32[]{:S(2)}) async-start(), calls=%async_computation.2 | async-start | bytes 2621440 | tf_op jit(solution)/shard_map/all_gather | solution.py:141
  8.7 176.3 %all-gather.13.cloned.1.call-start = ((), (), s32[]{:S(2)}) async-start(), calls=%async_computation.4 | async-start | bytes 5242880 | tf_op jit(solution)/shard_map/all_gather | solution.py:143
  9.4 256.3 %all-gather.15.cloned.1.call-start = ((), (), s32[]{:S(2)}) async-start(), calls=%async_computation.5 | async-start | bytes 5242880 | tf_op jit(solution)/shard_map/all_gather | solution.py:144
  10.0 1094.9 %all-gather.17.cloned.1.call-start = ((), (), s32[]{:S(2)}) async-start(), calls=%async_computation.6 | async-start | bytes 5242880 | tf_op jit(solution)/shard_map/all_gather | solution.py:145
  10.6 1100.2 %all-gather.19.cloned.1.call-start = ((), (), s32[]{:S(2)}) async-start(), calls=%async_computation.7 | async-start | bytes 7208960 | tf_op jit(solution)/shard_map/all_gather | solution.py:146
  11.2 1105.7 %all-gather.21.cloned.1.call-start = ((), (), s32[]{:S(2)}) async-start(), calls=%async_computation.8 | async-start | bytes 7208960 | tf_op jit(solution)/shard_map/all_gather | solution.py:147
  11.9 1111.0 %all-gather.23.cloned.1.call-start = ((), (), s32[]{:S(2)}) async-start(), calls=%async_computation.9 | async-start | bytes 7208960 | tf_op jit(solution)/shard_map/all_gather | solution.py:148
  12.7 2484.7 %reduce-scatter.3.cloned.1.call-start = ((), (), s32[]{:S(2)}) async-start(), calls=%async_computation.10 | async-start | bytes 41943040 | tf_op jit(solution)/shard_map/reduce_scatter | solution.py:256
  12.8 261.4 %copy-start.67 = (f32[1,4096]{1,0:T(1,128)}, f32[1,4096]{1,0:T(1,128)S(1)}, u32[]{:S(2)}) copy-start(f32[1,4096]{1,0:T(1,128)S(1)} %get-tuple-element.1162) | copy-start | bytes 49156
  12.8 261.4 %copy-start.69 = (f32[1,4096]{1,0:T(1,128)}, f32[1,4096]{1,0:T(1,128)S(1)}, u32[]{:S(2)}) copy-start(f32[1,4096]{1,0:T(1,128)S(1)} %get-tuple-element.1163) | copy-start | bytes 49156
  12.8 261.4 %copy-start.71 = (f32[1,4096]{1,0:T(1,128)}, f32[1,4096]{1,0:T(1,128)S(1)}, u32[]{:S(2)}) copy-start(f32[1,4096]{1,0:T(1,128)S(1)} %get-tuple-element.1164) | copy-start | bytes 49156
  12.9 261.4 %copy-start.73 = (f32[1,4096]{1,0:T(1,128)}, f32[1,4096]{1,0:T(1,128)S(1)}, u32[]{:S(2)}) copy-start(f32[1,4096]{1,0:T(1,128)S(1)} %get-tuple-element.1165) | copy-start | bytes 49156
  189.5 82.8 %collective-permute-start.2 = (bf16[2,3,4096]{2,1,0:T(4,128)(2,1)S(1)}, bf16[2,3,4096]{2,1,0:T(4,128)(2,1)S(1)}, u32[]{:S(2)}, u32[]{:S(2)}) collective-permute-start(bf16[2,3,4096]{2,1,0:T(4,128)(2,1)S(1)} %pad_maximum_fusion.2), channel_id=1, source_target_pairs={{0,4},{4,8},{8,12},{12,16},{16,20},{20,24},{24,28},{1,5},{5,9},{9,... | collective-permute-start | bytes 147464 | tf_op jit(solution)/shard_map/ppermute | solution.py:18
  666.6 26.9 collective-permute-start
  698.7 27.6 collective-permute-start
  731.4 27.6 collective-permute-start
  764.1 27.6 collective-permute-start
  796.7 27.6 collective-permute-start
  829.4 27.6 collective-permute-start
  862.1 27.6 collective-permute-start
  1361.2 28.2 collective-permute-start.1
  1394.5 27.6 collective-permute-start.1
  1427.2 27.6 collective-permute-start.1
  1459.8 27.6 collective-permute-start.1
  1492.5 27.6 collective-permute-start.1
  1525.2 27.6 collective-permute-start.1
  1557.9 27.6 collective-permute-start.1
  1895.3 7.0 collective-permute-start.3
  1935.3 1134.0 %reduce-scatter.5.cloned.1.call-start = ((), (), s32[]{:S(2)}) async-start(), calls=%async_computation.11 | async-start | bytes 43253760 | tf_op jit(solution)/shard_map/reduce_scatter | solution.py:214
  1978.3 1319.0 %all-reduce.19.cloned.1.call-start = ((), (), s32[]{:S(2)}) async-start(), calls=%async_computation.13 | async-start | bytes 34078720 | tf_op jit(solution)/shard_map/psum | solution.py:281
  3069.3 354.1 %all-reduce.17.cloned.1.call-start = ((), (), s32[]{:S(2)}) async-start(), calls=%async_computation.12 | async-start | bytes 131072 | tf_op jit(solution)/shard_map/psum | solution.py:282
  (117 other events, 956.2 us)
Sparse Core Ops, SparseCore 0:
  9.6 48.0 all-gather.10
  59.2 44.6 all-gather.8
  105.5 79.4 all-gather.12
  186.4 79.2 all-gather.14
  267.2 79.3 all-gather.16
  348.0 105.4 all-gather.18
  455.1 105.4 all-gather.20
  562.2 104.9 all-gather.22
  1935.4 561.8 reduce-scatter.2
  2499.7 569.5 reduce-scatter.4
  3073.9 223.3 all-reduce.18
  3304.2 119.1 all-reduce.16
where the time goes:
time: 3440 us; the launch traced here: 3430 us
  waiting for transfers between devices  1960 us (57%)
  other arithmetic  906 us (26%)
  matrix products  336 us (10%)
  local copies, waits for them, and re-layouts  114 us (3%)
  starting transfers between devices  49.6 us (1%)
  blocking collectives  43.4 us (1%)
    another operation x40, other arithmetic, group_step(): jax.scipy.linalg.solve_triangular(system, target, lower=True, unit_diagon...  803 us
    reduce_scatter x1, waiting for transfers between devices, shards(): lax.psum_scatter(jnp.concatenate([contract_rows(left_rows, d_gate), contr...  572 us
    reduce_scatter x1, waiting for transfers between devices, shards(): lax.psum_scatter(jnp.concatenate([contract_rows(left_rows, d_conv_flat),...  519 us
    ppermute x16, waiting for transfers between devices, passed_along(): return lax.ppermute(array, axis, pairs)  343 us
    psum x1, waiting for transfers between devices, shards(): mixer_sum, ffn_sum = lax.psum((mixer_share, ffn_share), 'seq')  167 us
    psum x1, waiting for transfers between devices, shards(): lax.psum((grad_beta, grad_conv, grad_in, middle_gradient, grad_head), ('s...  112 us
    all_gather x1, waiting for transfers between devices, shards(): lax.all_gather(w_value, 'wt', axis=0, tiled=True)  78.8 us
    all_gather x1, waiting for transfers between devices, shards(): lax.all_gather(w_gate_out, 'wt', axis=0, tiled=True)  72.1 us
  transfers between devices with their start and end apart: 28, of which 22 were waited for; matrix products, arithmetic and copies ran while one was open for 22% of the time, Pallas kernels for 0%

commit v1 on v0

--- a/solution.py
+++ b/solution.py
@@ -280,7 +280,7 @@
     grad_input = (d_residual + d_from_in).reshape(seq_count, block_len, model_width)
     mixer_sum, ffn_sum = lax.psum((mixer_share, ffn_share), "seq")
     grad_beta, grad_conv, grad_in, middle_gradient, grad_head = lax.psum(
-        (grad_beta, grad_conv, grad_in, middle_gradient, grad_head), ("seq", "wt")
+        lax.psum((grad_beta, grad_conv, grad_in, middle_gradient, grad_head), "wt"), "seq"
     )
     value_end = 2 * head_keys + head_values
     gate_end = value_end + head_values

time: 3440 us -> 3320 us (0.965)
  waiting for transfers between devices: 1960 us -> 1850 us
    psum x1, waiting for transfers between devices: 112 us -> 0.02 us  [shards(): lax.psum((grad_beta, grad_conv, grad_in, middle_gradient, grad_head), 'wt')]
  transfers between devices with their start and end apart: 28 -> 28, of which waited for: 22 -> 21; matrix products, arithmetic and copies ran while one was open for 22% -> 23% of each run, Pallas kernels for 0% -> 0%
where the time goes in v1:
time: 3320 us
  waiting for transfers between devices  1850 us (56%)
  other arithmetic  903 us (27%)
  matrix products  337 us (10%)
  local copies, waits for them, and re-layouts  110 us (3%)
  starting transfers between devices  49.4 us (1%)
  blocking collectives  43.2 us (1%)
    another operation x40, other arithmetic, group_step(): jax.scipy.linalg.solve_triangular(system, target, lower=True, unit_diagon...  803 us
    reduce_scatter x1, waiting for transfers between devices, shards(): lax.psum_scatter(jnp.concatenate([contract_rows(left_rows, d_gate), contr...  572 us
    reduce_scatter x1, waiting for transfers between devices, shards(): lax.psum_scatter(jnp.concatenate([contract_rows(left_rows, d_conv_flat),...  519 us
    ppermute x16, waiting for transfers between devices, passed_along(): return lax.ppermute(array, axis, pairs)  343 us
    psum x1, waiting for transfers between devices, shards(): mixer_sum, ffn_sum = lax.psum((mixer_share, ffn_share), 'seq')  169 us
    all_gather x1, waiting for transfers between devices, shards(): lax.all_gather(w_value, 'wt', axis=0, tiled=True)  78.8 us
    all_gather x1, waiting for transfers between devices, shards(): lax.all_gather(w_gate_out, 'wt', axis=0, tiled=True)  72.1 us
  transfers between devices with their start and end apart: 28, of which 21 were waited for; matrix products, arithmetic and copies ran while one was open for 23% of the time, Pallas kernels for 0%

profile of v1, /device:TPU:1, one launch (start us, length us, event | category | flops | bytes accessed | tf_op | source)
XLA Modules:
  0.0 3315.3 jit_solution(11363203493322535168)
XLA Ops:
  13.6 44.1 %all-gather.11.cloned.1.call-done = bf16[1024,1024]{1,0:T(8,128)(2,1)} async-done(((bf16[256,1024]{1,0:T(8,128)(2,1)}), bf16[1024,1024]{1,0:T(8,128)(2,1)}) %all-gather.11.cloned.1.call-update) | async-done | bytes 2097168 | tf_op jit(solution)/shard_map/all_gather | solution.py:142
  60.0 43.9 %all-gather.9.cloned.1.call-done = bf16[1024,1024]{1,0:T(8,128)(2,1)} async-done(((bf16[256,1024]{1,0:T(8,128)(2,1)}), bf16[1024,1024]{1,0:T(8,128)(2,1)}) %all-gather.9.cloned.1.call-update) | async-done | bytes 2097168 | tf_op jit(solution)/shard_map/all_gather | solution.py:141
  106.2 78.8 %all-gather.13.cloned.1.call-done = bf16[1024,2048]{1,0:T(8,128)(2,1)} async-done(((bf16[256,2048]{1,0:T(8,128)(2,1)}), bf16[1024,2048]{1,0:T(8,128)(2,1)}) %all-gather.13.cloned.1.call-update) | async-done | bytes 4194320 | tf_op jit(solution)/shard_map/all_gather | solution.py:143
  193.6 72.1 %all-gather.15.cloned.1.call-done = bf16[1024,2048]{1,0:T(8,128)(2,1)} async-done(((bf16[256,2048]{1,0:T(8,128)(2,1)}), bf16[1024,2048]{1,0:T(8,128)(2,1)}) %all-gather.15.cloned.1.call-update) | async-done | bytes 4194320 | tf_op jit(solution)/shard_map/all_gather | solution.py:144
  288.1 182.4 %while.96 = (s32[]{:T(128)}, f32[2,8,128,128]{3,2,1,0:T(8,128)}, f32[2,2,8,64]{3,2,1,0:T(8,128)S(1)}, f32[2,2,8,64,128]{4,3,2,1,0:T(8,128)S(1)}, f32[2,2,8,64]{3,2,1,0:T(8,128)S(1)}, /*index=5*/s32[]{:T(128)}, f32[]{:T(128)}) while((s32[]{:T(128)}, f32[2,8,128,128]{3,2,1,0:T(8,128)}, f32[2,2,8,64]{3,2,1,0:T(8,128)S(1)}, ...), condition=%wide.region_4.5_spmd, body=%wide.region_2.4_spmd.sunk | while | flops 605712448 | bytes 15951777 | solution.py:99
  293.8 80.0 %custom-call.36 = f32[2,8,1,64,64]{3,4,2,1,0:T(8,128)} custom-call(f32[2,8,1,64,64]{4,3,2,1,0:T(8,128)} %fusion.427), custom_call_target="InvertDiagBlocksLowerTriangular" | custom-call | tf_op jit(solution)/shard_map/vmap()/while/body/eval_jaxpr/checkpoint/jit(_solve_triangular)/vmap()/triangular_solve | solution.py:80
  384.9 80.0 %custom-call.36 = f32[2,8,1,64,64]{3,4,2,1,0:T(8,128)} custom-call(f32[2,8,1,64,64]{4,3,2,1,0:T(8,128)} %fusion.427), custom_call_target="InvertDiagBlocksLowerTriangular" | custom-call | tf_op jit(solution)/shard_map/vmap()/while/body/eval_jaxpr/checkpoint/jit(_solve_triangular)/vmap()/triangular_solve | solution.py:80
  474.9 183.1 %while.101 = (s32[]{:T(128)}, f32[2,8,128,256]{3,2,1,0:T(8,128)S(1)}, f32[2,2,8,64]{3,2,1,0:T(8,128)S(1)}, f32[2,2,8,64,128]{4,3,2,1,0:T(8,128)S(1)}, f32[2,2,8,...) while((s32[]{:T(128)}, ...), condition=%wide.region_7.9_spmd.clone, body=%wide.region_5.8_spmd.clone.sunk | while | flops 1110994944 | bytes 13856127 | solution.py:99
  481.4 80.0 %custom-call.39 = f32[2,8,1,64,64]{3,4,2,1,0:T(8,128)} custom-call(f32[2,8,1,64,64]{4,3,2,1,0:T(8,128)} %fusion.505), custom_call_target="InvertDiagBlocksLowerTriangular" | custom-call | tf_op jit(solution)/shard_map/vmap()/while/body/eval_jaxpr/checkpoint/jit(_solve_triangular)/vmap()/triangular_solve/custom-call.0 | solution.py:80
  572.9 80.0 %custom-call.39 = f32[2,8,1,64,64]{3,4,2,1,0:T(8,128)} custom-call(f32[2,8,1,64,64]{4,3,2,1,0:T(8,128)} %fusion.505), custom_call_target="InvertDiagBlocksLowerTriangular" | custom-call | tf_op jit(solution)/shard_map/vmap()/while/body/eval_jaxpr/checkpoint/jit(_solve_triangular)/vmap()/triangular_solve/custom-call.0 | solution.py:80
  661.5 228.1 %while.97 = (s32[]{:T(128)}, f32[2,8,128,256]{3,2,1,0:T(8,128)S(1)}, f32[2,8,128,128]{3,2,1,0:T(8,128)}, f32[2,8,128,256]{3,2,1,0:T(8,128)}, s32[]{:T(128)}) while((s32[]{:T(128)}, f32[2,8,128,256]{3,2,1,0:T(8,128)S(1)}, f32[2,8,128,128]{3,2,1,0:T(8,128)}, f32[2,8,128,256]{3,2,1,0:T(8,128)}, s32[]{:T(128)}) %tuple.364), condition=%wide.region_9.11_spmd, body=%wide.region_8.10_spmd.sunk | while | flops 805830656 | bytes 15728741 | solution.py:182
  891.2 199.9 %while.100 = (s32[]{:T(128)}, f32[2,8,128,256]{3,2,1,0:T(8,128)S(1)}, f32[2,2,8,64,256]{4,3,2,1,0:T(8,128)}, f32[2,2,8,128,256]{4,3,2,1,0:T(8,128)}, f32[2,2,8,6...) while((s32[]{:T(128)}, ...), condition=%wide.region_12.14_spmd.clone.clone, body=%wide.region_10.13_spmd.clone.clone.sunk | while | flops 1815367680 | bytes 56082448 | solution.py:99
  901.6 80.0 %custom-call.38 = f32[2,8,1,64,64]{3,4,2,1,0:T(8,128)} custom-call(f32[2,8,1,64,64]{4,3,2,1,0:T(8,128)} %fusion.494), custom_call_target="InvertDiagBlocksLowerTriangular" | custom-call | tf_op jit(solution)/shard_map/jvp(vmap())/while/body/eval_jaxpr/jit(_solve_triangular)/vmap()/triangular_solve/custom-call.0 | solution.py:80
  1001.3 80.0 %custom-call.38 = f32[2,8,1,64,64]{3,4,2,1,0:T(8,128)} custom-call(f32[2,8,1,64,64]{4,3,2,1,0:T(8,128)} %fusion.494), custom_call_target="InvertDiagBlocksLowerTriangular" | custom-call | tf_op jit(solution)/shard_map/jvp(vmap())/while/body/eval_jaxpr/jit(_solve_triangular)/vmap()/triangular_solve/custom-call.0 | solution.py:80
  1148.8 206.4 %while.102 = (s32[]{:T(128)}, f32[2,8,128,256]{3,2,1,0:T(8,128)}, f32[2,2,8,64,128]{4,3,2,1,0:T(8,128)}, f32[2,2,8,64,128]{4,3,2,1,0:T(8,128)S(1)}, f32[2,2,8,64...) while((s32[]{:T(128)}, f32[2,8,128,256]{3,2,1,0:T(8,128)}, ...), condition=%wide.region_19.22_spmd.clone, body=%wide.region_17.21_spmd.clone.sunk | while | flops 1816424448 | bytes 58881144 | solution.py:99
  1165.4 80.0 %custom-call.40 = f32[2,8,1,64,64]{3,4,2,1,0:T(8,128)} custom-call(f32[2,8,1,64,64]{4,3,2,1,0:T(8,128)} %fusion.524), custom_call_target="InvertDiagBlocksLowerTriangular" | custom-call | tf_op jit(solution)/shard_map/transpose(jvp(vmap()))/while/body/eval_jaxpr/checkpoint/jit(_solve_triangular)/vmap()/triangular_solve/custom-call.2 | solution.py:80
  1268.9 80.0 %custom-call.40 = f32[2,8,1,64,64]{3,4,2,1,0:T(8,128)} custom-call(f32[2,8,1,64,64]{4,3,2,1,0:T(8,128)} %fusion.524), custom_call_target="InvertDiagBlocksLowerTriangular" | custom-call | tf_op jit(solution)/shard_map/transpose(jvp(vmap()))/while/body/eval_jaxpr/checkpoint/jit(_solve_triangular)/vmap()/triangular_solve/custom-call.2 | solution.py:80
  1355.5 229.9 %while.98 = (s32[]{:T(128)}, f32[2,8,128,256]{3,2,1,0:T(8,128)S(1)}, f32[2,8,128,128]{3,2,1,0:T(8,128)}, f32[2,8,128,256]{3,2,1,0:T(8,128)}, s32[]{:T(128)}) while((s32[]{:T(128)}, f32[2,8,128,256]{3,2,1,0:T(8,128)S(1)}, f32[2,8,128,128]{3,2,1,0:T(8,128)}, f32[2,8,128,256]{3,2,1,0:T(8,128)}, s32[]{:T(128)}) %tuple.370), condition=%wide.region_21.24_spmd, body=%wide.region_20.23_spmd.sunk | while | flops 805830656 | bytes 15728741 | solution.py:242
  1363.0 26.3 collective-permute-done.1
  1396.3 25.6 collective-permute-done.1
  1429.0 25.6 collective-permute-done.1
  1461.7 25.6 collective-permute-done.1
  1494.3 25.6 collective-permute-done.1
  1527.0 25.6 collective-permute-done.1
  1559.7 25.6 collective-permute-done.1
  1589.1 255.9 %while.99 = (s32[]{:T(128)}, f32[2,8,128,256]{3,2,1,0:T(8,128)S(1)}, f32[2,2,8,64,128]{4,3,2,1,0:T(8,128)}, f32[2,2,8,64,128]{4,2,3,0,1:T(8,128)}, f32[2,2,8,64,...) while((s32[]{:T(128)}, ...), condition=%wide.region_26.29_spmd, body=%wide.region_22.28_spmd.sunk | while | flops 4487867392 | bytes 149161456 | solution.py:99
  1603.9 80.0 %custom-call.37 = f32[2,8,1,64,64]{3,4,2,1,0:T(8,128)} custom-call(f32[2,8,1,64,64]{4,3,2,1,0:T(8,128)} %add_bitcast_fusion.2), custom_call_target="InvertDiagBlocksLowerTriangular" | custom-call | tf_op jit(solution)/shard_map/transpose(jvp(vmap()))/while/body/eval_jaxpr/checkpoint/jit(_solve_triangular)/vmap()/triangular_solve/custom-call.2 | solution.py:80
  1727.8 80.0 %custom-call.37 = f32[2,8,1,64,64]{3,4,2,1,0:T(8,128)} custom-call(f32[2,8,1,64,64]{4,3,2,1,0:T(8,128)} %add_bitcast_fusion.2), custom_call_target="InvertDiagBlocksLowerTriangular" | custom-call | tf_op jit(solution)/shard_map/transpose(jvp(vmap()))/while/body/eval_jaxpr/checkpoint/jit(_solve_triangular)/vmap()/triangular_solve/custom-call.2 | solution.py:80
  1974.8 518.6 %reduce-scatter.3.cloned.1.call-done = f32[256,8192]{1,0:T(8,128)} async-done(((f32[1024,8192]{1,0:T(8,128)}), f32[256,8192]{1,0:T(8,128)}) %reduce-scatter.3.cloned.1.call-update) | async-done | bytes 8388624 | tf_op jit(solution)/shard_map/reduce_scatter | solution.py:256
  2493.4 572.0 %reduce-scatter.5.cloned.1.call-done = f32[256,8448]{1,0:T(8,128)} async-done(((f32[1024,8448]{1,0:T(8,128)}), f32[256,8448]{1,0:T(8,128)}) %reduce-scatter.5.cloned.1.call-update) | async-done | bytes 8650768 | tf_op jit(solution)/shard_map/reduce_scatter | solution.py:214
  3095.8 27.4 all-reduce.12
  3124.4 168.8 %all-reduce.20.cloned.1.call-done = (f32[256,8192]{1,0:T(8,128)}, f32[256,8448]{1,0:T(8,128)}, f32[4,4096]{1,0:T(4,128)}) async-done(((f32[256,8192]{1,0:T(8,128)}, f32[256,8448]{1,0:T(8,128)}, f32[4,4096]{1,0:T(4,128)}), (f32[256,8192]{1,0:T(8,128)}, f32[256,8448]{1,0:T(8,128)}, f32[4,4096]{1,0:T(4,128)})) %all-reduce.20.cloned.1.call-update) | async-done | bytes 17104912 | tf_op jit(solution)/shard_map/psum | solution.py:281
  (616 shorter events, 783.3 us)
Async XLA Ops:
  7.2 50.5 %all-gather.11.cloned.1.call-start = ((), (), s32[]{:S(2)}) async-start(), calls=%async_computation.3 | async-start | bytes 2621440 | tf_op jit(solution)/shard_map/all_gather | solution.py:142
  7.9 96.0 %all-gather.9.cloned.1.call-start = ((), (), s32[]{:S(2)}) async-start(), calls=%async_computation.2 | async-start | bytes 2621440 | tf_op jit(solution)/shard_map/all_gather | solution.py:141
  8.7 176.3 %all-gather.13.cloned.1.call-start = ((), (), s32[]{:S(2)}) async-start(), calls=%async_computation.4 | async-start | bytes 5242880 | tf_op jit(solution)/shard_map/all_gather | solution.py:143
  9.4 256.3 %all-gather.15.cloned.1.call-start = ((), (), s32[]{:S(2)}) async-start(), calls=%async_computation.5 | async-start | bytes 5242880 | tf_op jit(solution)/shard_map/all_gather | solution.py:144
  10.0 1094.9 %all-gather.17.cloned.1.call-start = ((), (), s32[]{:S(2)}) async-start(), calls=%async_computation.6 | async-start | bytes 5242880 | tf_op jit(solution)/shard_map/all_gather | solution.py:145
  10.6 1100.2 %all-gather.19.cloned.1.call-start = ((), (), s32[]{:S(2)}) async-start(), calls=%async_computation.7 | async-start | bytes 7208960 | tf_op jit(solution)/shard_map/all_gather | solution.py:146
  11.2 1105.7 %all-gather.21.cloned.1.call-start = ((), (), s32[]{:S(2)}) async-start(), calls=%async_computation.8 | async-start | bytes 7208960 | tf_op jit(solution)/shard_map/all_gather | solution.py:147
  11.9 1111.0 %all-gather.23.cloned.1.call-start = ((), (), s32[]{:S(2)}) async-start(), calls=%async_computation.9 | async-start | bytes 7208960 | tf_op jit(solution)/shard_map/all_gather | solution.py:148
  12.7 1962.1 %all-reduce.18.cloned.1.call-start = ((), (), s32[]{:S(2)}) async-start(), calls=%async_computation.12 | async-start | bytes 131072 | tf_op jit(solution)/shard_map/psum | solution.py:283
  12.8 261.4 %copy-start.69 = (f32[1,4096]{1,0:T(1,128)}, f32[1,4096]{1,0:T(1,128)S(1)}, u32[]{:S(2)}) copy-start(f32[1,4096]{1,0:T(1,128)S(1)} %get-tuple-element.1167) | copy-start | bytes 49156
  12.8 261.4 %copy-start.71 = (f32[1,4096]{1,0:T(1,128)}, f32[1,4096]{1,0:T(1,128)S(1)}, u32[]{:S(2)}) copy-start(f32[1,4096]{1,0:T(1,128)S(1)} %get-tuple-element.1168) | copy-start | bytes 49156
  12.8 261.4 %copy-start.73 = (f32[1,4096]{1,0:T(1,128)}, f32[1,4096]{1,0:T(1,128)S(1)}, u32[]{:S(2)}) copy-start(f32[1,4096]{1,0:T(1,128)S(1)} %get-tuple-element.1169) | copy-start | bytes 49156
  12.9 261.4 %copy-start.75 = (f32[1,4096]{1,0:T(1,128)}, f32[1,4096]{1,0:T(1,128)S(1)}, u32[]{:S(2)}) copy-start(f32[1,4096]{1,0:T(1,128)S(1)} %get-tuple-element.1170) | copy-start | bytes 49156
  189.5 82.8 %collective-permute-start.2 = (bf16[2,3,4096]{2,1,0:T(4,128)(2,1)S(1)}, bf16[2,3,4096]{2,1,0:T(4,128)(2,1)S(1)}, u32[]{:S(2)}, u32[]{:S(2)}) collective-permute-start(bf16[2,3,4096]{2,1,0:T(4,128)(2,1)S(1)} %pad_maximum_fusion.2), channel_id=1, source_target_pairs={{0,4},{4,8},{8,12},{12,16},{16,20},{20,24},{24,28},{1,5},{5,9},{9,... | collective-permute-start | bytes 147464 | tf_op jit(solution)/shard_map/ppermute | solution.py:18
  666.6 26.9 collective-permute-start
  698.7 27.6 collective-permute-start
  731.4 27.6 collective-permute-start
  764.1 27.6 collective-permute-start
  796.7 27.6 collective-permute-start
  829.4 27.6 collective-permute-start
  862.1 27.6 collective-permute-start
  1361.1 28.2 collective-permute-start.1
  1394.4 27.6 collective-permute-start.1
  1427.1 27.6 collective-permute-start.1
  1459.7 27.6 collective-permute-start.1
  1492.4 27.6 collective-permute-start.1
  1525.1 27.6 collective-permute-start.1
  1557.8 27.6 collective-permute-start.1
  1892.3 7.5 collective-permute-start.3
  1895.0 598.4 %reduce-scatter.3.cloned.1.call-start = ((), (), s32[]{:S(2)}) async-start(), calls=%async_computation.10 | async-start | bytes 41943040 | tf_op jit(solution)/shard_map/reduce_scatter | solution.py:256
  1931.6 1133.8 %reduce-scatter.5.cloned.1.call-start = ((), (), s32[]{:S(2)}) async-start(), calls=%async_computation.11 | async-start | bytes 43253760 | tf_op jit(solution)/shard_map/reduce_scatter | solution.py:214
  1974.5 1318.7 %all-reduce.20.cloned.1.call-start = ((), (), s32[]{:S(2)}) async-start(), calls=%async_computation.13 | async-start | bytes 34209792 | tf_op jit(solution)/shard_map/psum | solution.py:281
  (120 other events, 1017.9 us)
Sparse Core Ops, SparseCore 0:
  9.6 48.0 all-gather.10
  59.2 44.6 all-gather.8
  105.5 79.4 all-gather.12
  186.4 79.2 all-gather.14
  267.2 79.3 all-gather.16
  348.0 105.4 all-gather.18
  455.1 105.4 all-gather.20
  562.2 104.9 all-gather.22
  1895.1 41.9 all-reduce.17
  1939.4 553.9 reduce-scatter.2
  2495.8 569.5 reduce-scatter.4
  3069.5 223.7 all-reduce.19
